TPU v7x, 256 devices: a whole 4x4x8 slice. The times are simulated.
256 devices in a mesh: slab: 16 (over y, x), mode: 16 (over z, core).
Axes of the slice: x: 4, y: 4, z: 8, core: 2. Of those that a mesh axis runs over, the one named last changes fastest.
Arguments:
- tensor: bfloat16 [512, 131072], P('mode', 'slab'), may hold values from -24 to 24, as said below
- start_block: float32 [512, 128], replicated, may hold values from -6 to 6
Outputs:
- basis_rows: float32 [512, 128], P('mode')
- core_coeffs: float32 [131072, 128], P(('slab', 'mode'))
Inputs may be any that keep to these rules, and one draw needn't show every extreme that they name: `tensor`: entries of the unfolding; each is a row factor times a column factor times a bounded random term.
All inputs are finite; a program needn't handle non-finite values.
Results may differ from a plain program's by a relative error of at most 0.0029.
Values may be sent and summed in bfloat16 or wider, within the bound.
A program may use at most 64 MiB of HBM per device.

v0:
```python
import jax
import jax.numpy as jnp
from jax import lax
from jax.sharding import PartitionSpec as P

highest = lax.Precision.HIGHEST
contract_cols = (((1,), (1,)), ((), ()))
contract_rows = (((0,), (0,)), ((), ()))


def orthonormal(image_block):
    small_gram = jnp.dot(image_block.T, image_block, precision=highest)
    factor = jnp.linalg.cholesky(small_gram)
    return lax.linalg.triangular_solve(
        factor, image_block, left_side=False, lower=True, transpose_a=True
    )


def shards(tensor, start_block):
    row_count = tensor.shape[0]
    mode_index = lax.axis_index("mode")
    regrouped = lax.all_to_all(tensor, "mode", split_axis=1, concat_axis=0, tiled=True)
    local_gram = lax.dot_general(
        regrouped, regrouped, contract_cols, preferred_element_type=jnp.float32
    )
    gram_total = lax.psum(local_gram, ("slab", "mode"))
    image_block = jnp.dot(gram_total, start_block, precision=highest)
    basis_full = orthonormal(image_block)
    basis_low = basis_full.astype(jnp.bfloat16)
    basis_rows = lax.dynamic_slice_in_dim(basis_full, mode_index * row_count, row_count, 0)
    core_coeffs = lax.dot_general(
        regrouped, basis_low, contract_rows, preferred_element_type=jnp.float32
    )
    return (basis_rows, core_coeffs)


def solution(mesh):
    placed = (P("mode", "slab"), P())
    return jax.shard_map(
        shards,
        mesh=mesh,
        in_specs=placed,
        out_specs=(P("mode", None), P(("slab", "mode"), None)),
        check_vma=False,
    )
```

profile of v0, /device:TPU:2, one launch (start us, length us, event | category | flops | bytes accessed | tf_op | source)
XLA Modules:
  0.0 326.6 jit_solution(6227881989262356702)
XLA Ops:
  7.2 0.0 copy-start
  7.2 0.0 all-reduce.2.cloned.1.call-start
  7.2 1.1 copy.16
  8.4 24.3 %all_to_all.19 = bf16[32,16,512]{2,0,1:T(8,128)(2,1)S(1)} all-to-all(bf16[32,16,512]{2,0,1:T(8,128)(2,1)S(1)} %bitcast.28), channel_id=1, replica_groups=mesh['slab'=16,'mode'=16] {'mode'}, dimensions={1} | all-to-all | bytes 1048576 | tf_op jit(solution)/shard_map/all_to_all | solution.py:22
  32.7 1.5 fusion.5
  34.2 0.0 all-reduce.2.cloned.1.call-update
  34.2 257.6 %all-reduce.2.cloned.1.call-done = f32[512,512]{1,0:T(8,128)} async-done(((f32[512,512]{1,0:T(8,128)}), f32[512,512]{1,0:T(8,128)}) %all-reduce.2.cloned.1.call-update) | async-done | bytes 1048592 | tf_op jit(solution)/shard_map/psum | solution.py:26
  291.8 0.0 copy-done
  291.9 2.2 fusion.6
  294.1 0.6 fusion.7
  294.7 0.1 copy.12
  294.8 11.7 %cholesky.16 = f32[128,128]{1,0:T(8,128)S(1)} custom-call(f32[128,128]{1,0:T(8,128)S(1)} %fusion.4), custom_call_target="Cholesky" | custom-call | tf_op jit(solution)/shard_map/jit(cholesky)/cholesky | solution.py:13
  306.5 0.6 compare_reduce_fusion
  307.2 0.7 fusion.1
  307.8 9.8 %custom-call.6 = f32[1,128,128]{1,2,0:T(8,128)S(1)} custom-call(f32[1,128,128]{2,1,0:T(8,128)S(1)} %fusion.1), custom_call_target="InvertDiagBlocksLowerTriangular" | custom-call | tf_op jit(solution)/shard_map/triangular_solve | solution.py:14
  317.6 0.4 fusion.2
  318.0 0.3 convolution_bitcast_fusion
  318.3 0.6 constant_dynamic-slice_fusion
  318.9 0.8 copy.13
  (2 shorter events, 0.0 us)
Async XLA Ops:
  7.2 284.7 %copy-start = (f32[512,128]{1,0:T(8,128)S(1)}, f32[512,128]{1,0:T(8,128)}, u32[]{:S(2)}) copy-start(f32[512,128]{1,0:T(8,128)} %param.3) | copy-start | bytes 786436
  7.2 284.7 %all-reduce.2.cloned.1.call-start = ((), (), s32[]{:S(2)}) async-start(), calls=%async_computation.1 | async-start | bytes 2097152 | tf_op jit(solution)/shard_map/psum | solution.py:26
Sparse Core Ops, SparseCore 0:
  34.3 257.4 all-reduce.1
where the time goes:
time: 327 us
  waiting for transfers between devices  258 us (79%)
  blocking collectives  24.3 us (7%)
  other arithmetic  22.9 us (7%)
  between operations  14.1 us (4%)
  matrix products  4.92 us (2%)
    psum x1, waiting for transfers between devices, shards(): gram_total = lax.psum(local_gram, ('slab', 'mode'))  258 us
    all_to_all x1, blocking collectives, shards(): lax.all_to_all(tensor, 'mode', split_axis=1, concat_axis=0, tiled=True)  24.3 us
    another operation x3, other arithmetic, orthonormal(): factor = jnp.linalg.cholesky(small_gram)  12.4 us
    another operation x2, other arithmetic, orthonormal(): lax.linalg.triangular_solve(factor, image_block, left_side=False, lower=T...  10.5 us
  transfers between devices with their start and end apart: 1, of which 1 were waited for; matrix products, arithmetic and copies ran while one was open for 0% of the time, Pallas kernels for 0%

commit v1 on v0

--- a/solution.py
+++ b/solution.py
@@ -2,6 +2,7 @@
 import jax.numpy as jnp
 from jax import lax
 from jax.sharding import PartitionSpec as P
+from jax.lax import psum
 
 highest = lax.Precision.HIGHEST
 contract_cols = (((1,), (1,)), ((), ()))
@@ -23,7 +24,9 @@
     local_gram = lax.dot_general(
         regrouped, regrouped, contract_cols, preferred_element_type=jnp.float32
     )
-    gram_total = lax.psum(local_gram, ("slab", "mode"))
+    gram_total = local_gram
+    for it in ("slab", "mode"):
+        gram_total = psum(gram_total, axis_name=it)
     image_block = jnp.dot(gram_total, start_block, precision=highest)
     basis_full = orthonormal(image_block)
     basis_low = basis_full.astype(jnp.bfloat16)

time: 327 us -> 280 us (0.86)
  waiting for transfers between devices: 258 us -> 210 us
    psum x1 -> x2, waiting for transfers between devices: 258 us -> 210 us  [shards(): gram_total = psum(gram_total, axis_name=it)]
  transfers between devices with their start and end apart: 1 -> 2, of which waited for: 1 -> 2; matrix products, arithmetic and copies ran while one was open for 0% -> 0% of each run, Pallas kernels for 0% -> 0%
where the time goes in v1:
time: 280 us; the launch traced here: 279 us
  waiting for transfers between devices  210 us (75%)
  blocking collectives  24.3 us (9%)
  other arithmetic  22.9 us (8%)
  between operations  14.1 us (5%)
  matrix products  4.92 us (2%)
    psum x2, waiting for transfers between devices, shards(): gram_total = psum(gram_total, axis_name=it)  210 us
    all_to_all x1, blocking collectives, shards(): lax.all_to_all(tensor, 'mode', split_axis=1, concat_axis=0, tiled=True)  24.3 us
    another operation x3, other arithmetic, orthonormal(): factor = jnp.linalg.cholesky(small_gram)  12.4 us
    another operation x2, other arithmetic, orthonormal(): lax.linalg.triangular_solve(factor, image_block, left_side=False, lower=T...  10.5 us
  transfers between devices with their start and end apart: 2, of which 2 were waited for; matrix products, arithmetic and copies ran while one was open for 0% of the time, Pallas kernels for 0%

profile of v1, /device:TPU:2, one launch (start us, length us, event | category | flops | bytes accessed | tf_op | source)
XLA Modules:
  0.0 279.2 jit_solution(15212552196799486240)
XLA Ops:
  7.2 0.0 copy-start
  7.2 0.0 all-reduce.3.cloned.1.call-start
  7.2 1.1 copy.16
  8.4 24.3 %all_to_all.19 = bf16[32,16,512]{2,0,1:T(8,128)(2,1)S(1)} all-to-all(bf16[32,16,512]{2,0,1:T(8,128)(2,1)S(1)} %bitcast.28), channel_id=1, replica_groups=mesh['slab'=16,'mode'=16] {'mode'}, dimensions={1} | all-to-all | bytes 1048576 | tf_op jit(solution)/shard_map/all_to_all | solution.py:23
  32.7 1.5 fusion.5
  34.2 0.0 all-reduce.3.cloned.1.call-update
  34.2 0.0 all-reduce.5.cloned.1.call-start
  34.2 95.6 %all-reduce.3.cloned.1.call-done = f32[512,512]{1,0:T(8,128)} async-done(((f32[512,512]{1,0:T(8,128)}), f32[512,512]{1,0:T(8,128)}) %all-reduce.3.cloned.1.call-update) | async-done | bytes 1048592 | tf_op jit(solution)/shard_map/psum | solution.py:29
  129.9 0.0 all-reduce.5.cloned.1.call-update
  129.9 114.6 %all-reduce.5.cloned.1.call-done = f32[512,512]{1,0:T(8,128)} async-done(((f32[512,512]{1,0:T(8,128)}), f32[512,512]{1,0:T(8,128)}) %all-reduce.5.cloned.1.call-update) | async-done | bytes 1048592 | tf_op jit(solution)/shard_map/psum | solution.py:29
  244.5 0.0 copy-done
  244.5 2.2 fusion.6
  246.7 0.6 fusion.7
  247.3 0.1 copy.12
  247.4 11.7 %cholesky.16 = f32[128,128]{1,0:T(8,128)S(1)} custom-call(f32[128,128]{1,0:T(8,128)S(1)} %fusion.4), custom_call_target="Cholesky" | custom-call | tf_op jit(solution)/shard_map/jit(cholesky)/cholesky | solution.py:14
  259.1 0.6 compare_reduce_fusion
  259.8 0.7 fusion.1
  260.5 9.8 %custom-call.6 = f32[1,128,128]{1,2,0:T(8,128)S(1)} custom-call(f32[1,128,128]{2,1,0:T(8,128)S(1)} %fusion.1), custom_call_target="InvertDiagBlocksLowerTriangular" | custom-call | tf_op jit(solution)/shard_map/triangular_solve | solution.py:15
  270.3 0.4 fusion.2
  270.6 0.3 convolution_bitcast_fusion
  270.9 0.6 constant_dynamic-slice_fusion
  271.5 0.8 copy.13
  (2 shorter events, 0.0 us)
Async XLA Ops:
  7.2 237.3 %copy-start = (f32[512,128]{1,0:T(8,128)S(1)}, f32[512,128]{1,0:T(8,128)}, u32[]{:S(2)}) copy-start(f32[512,128]{1,0:T(8,128)} %param.3) | copy-start | bytes 786436
  7.2 122.7 %all-reduce.3.cloned.1.call-start = ((), (), s32[]{:S(2)}) async-start(), calls=%async_computation.1 | async-start | bytes 2097152 | tf_op jit(solution)/shard_map/psum | solution.py:29
  34.2 210.3 %all-reduce.5.cloned.1.call-start = ((), (), s32[]{:S(2)}) async-start(), calls=%async_computation.2 | async-start | bytes 2097152 | tf_op jit(solution)/shard_map/psum | solution.py:29
Sparse Core Ops, SparseCore 0:
  34.3 95.5 all-reduce.2
  132.2 112.2 all-reduce.4
